TPU v7x, 32 devices: a whole 2x2x4 slice. The times are simulated.
32 devices in a mesh: gx: 4 (over y, core), gy: 8 (over z, x).
Axes of the slice: x: 2, y: 2, z: 4, core: 2. Of those that a mesh axis runs over, the one named last changes fastest.
Arguments:
- hidden: bfloat16 [256, 8192], P('gx', 'gy'), may hold values from -12 to 12
- lengths: int32 [256], P('gy'), may hold values from 1 to 384
- draft_ids: int32 [256], P('gy'), may hold values from 0 to 31999
- attn_gain: bfloat16 [8192], P('gy'), may hold values from 0.099609375 to 1.8984375
- w_query: bfloat16 [8192, 8192], P('gy', 'gx'), may hold values from -0.0625 to 0.0625
- w_key: bfloat16 [8192, 1024], P('gy', 'gx'), may hold values from -0.0625 to 0.0625
- w_value: bfloat16 [8192, 1024], P('gy', 'gx'), may hold values from -0.0625 to 0.0625
- w_out: bfloat16 [8192, 8192], P('gx', 'gy'), may hold values from -0.0625 to 0.0625
- cache_k: bfloat16 [256, 8, 384, 128], P('gy', 'gx'), may hold values from -240 to 240
- cache_v: bfloat16 [256, 8, 384, 128], P('gy', 'gx'), may hold values from -6 to 6
- mlp_gain: bfloat16 [8192], P('gy'), may hold values from 0.099609375 to 1.8984375
- w_gate: bfloat16 [8192, 28672], P('gy', 'gx'), may hold values from -0.0625 to 0.0625
- w_up: bfloat16 [8192, 28672], P('gy', 'gx'), may hold values from -0.0625 to 0.0625
- w_down: bfloat16 [28672, 8192], P('gx', 'gy'), may hold values from -0.03125 to 0.03125
- final_gain: bfloat16 [8192], P('gy'), may hold values from 0.099609375 to 1.8984375
- w_head: bfloat16 [8192, 32000], P('gy', 'gx'), may hold values from -1 to 1
Outputs:
- log_probs: float32 [256, 32000], P('gy', 'gx')
- draft_logprob: float32 [256], P('gy')
All inputs are finite; a program needn't handle non-finite values.
Results may differ from a plain program's by a relative error of at most 0.002.
Values may be sent and summed in bfloat16 or wider, within the bound.
No kernel may reach another device: no remote copies, remote signals or barrier semaphores. Data moves between devices by JAX's collectives and lax.ppermute only.
A program may use at most 192 MiB of HBM per device.

v0:
```python
import jax
import jax.numpy as jnp
from jax import lax
from jax.sharding import PartitionSpec as P

D = 8192
HEAD_DIM = 128
epsilon = 1e-05


def combined_all(x, axis, combine):
    everything = jax.tree.map(lambda part: lax.all_gather(part, axis), x)
    initial = jax.tree.map(lambda part: part[0], everything)

    def step(k, so_far):
        return combine(so_far, jax.tree.map(lambda part: part[k], everything))

    return lax.fori_loop(1, lax.axis_size(axis), step, initial)


def rotate(vectors, position):
    half_dim = vectors.shape[-1] // 2
    frequency = jnp.exp(
        -jnp.log(10000.0) * jnp.arange(half_dim, dtype=jnp.float32) * (2.0 / vectors.shape[-1])
    )
    angle_table = position[:, None, None] * frequency
    cosine = jnp.cos(angle_table)
    sine_part = jnp.sin(angle_table)
    first_half = vectors[..., :half_dim]
    second_half = vectors[..., half_dim:]
    return jnp.concatenate(
        [
            first_half * cosine - second_half * sine_part,
            second_half * cosine + first_half * sine_part,
        ],
        axis=-1,
    )


def normalize_rows(activity, gain_row):
    squares = lax.psum(jnp.sum(activity * activity, axis=1), "gy")
    factor = lax.rsqrt(squares / D + epsilon)
    normed = (activity * factor[:, None] * gain_row.astype(jnp.float32)).astype(jnp.bfloat16)
    return lax.all_gather(normed, "gx", axis=0, tiled=True)


def attend_one(queries, own_key, own_value, cached_keys, values, usable):
    scaling = queries.shape[-1] ** (-0.5)
    scores = (
        jnp.einsum("bgd,btd->bgt", queries, cached_keys, preferred_element_type=jnp.float32)
        * scaling
    )
    own_score = (
        jnp.einsum("bgd,bd->bg", queries, own_key, preferred_element_type=jnp.float32) * scaling
    )
    scores = jnp.where(usable[:, None, :], scores, -jnp.inf)
    highest = jnp.maximum(jnp.max(scores, axis=2), own_score)
    weights = jnp.exp(scores - highest[:, :, None])
    own_weight = jnp.exp(own_score - highest)
    denominator = jnp.sum(weights, axis=2) + own_weight
    weights = (weights / denominator[:, :, None]).astype(jnp.bfloat16)
    own_weight = (own_weight / denominator).astype(jnp.bfloat16)
    blended = jnp.einsum("bgt,btd->bgd", weights, values, preferred_element_type=jnp.float32)
    blended = (
        blended
        + own_weight.astype(jnp.float32)[:, :, None] * own_value.astype(jnp.float32)[:, None, :]
    )
    return blended.astype(jnp.bfloat16)


def combine_totals(former, latter):
    highest = jnp.maximum(former[0], latter[0])
    summed = former[1] * jnp.exp(former[0] - highest) + latter[1] * jnp.exp(latter[0] - highest)
    return (highest, summed, former[2] + latter[2])


def shards(
    hidden,
    lengths,
    draft_ids,
    attn_gain,
    w_query,
    w_key,
    w_value,
    w_out,
    cache_k,
    cache_v,
    mlp_gain,
    w_gate,
    w_up,
    w_down,
    final_gain,
    w_head,
):
    residual = hidden.astype(jnp.float32)
    tokens = normalize_rows(residual, attn_gain)
    row_slab = tokens
    projected = lax.psum_scatter(
        jnp.concatenate(
            [
                jnp.dot(row_slab, w_query, preferred_element_type=jnp.float32),
                jnp.dot(row_slab, w_key, preferred_element_type=jnp.float32),
                jnp.dot(row_slab, w_value, preferred_element_type=jnp.float32),
            ],
            axis=1,
        ),
        "gy",
        scatter_dimension=0,
        tiled=True,
    )
    query_width = w_query.shape[1]
    key_width = w_key.shape[1]
    local_rows = projected.shape[0]
    position = lengths.astype(jnp.float32)
    queries = rotate(projected[:, :query_width].reshape(local_rows, -1, HEAD_DIM), position).astype(
        jnp.bfloat16
    )
    new_keys = rotate(
        projected[:, query_width : query_width + key_width].reshape(local_rows, -1, HEAD_DIM),
        position,
    ).astype(jnp.bfloat16)
    new_values = (
        projected[:, query_width + key_width :]
        .reshape(local_rows, -1, HEAD_DIM)
        .astype(jnp.bfloat16)
    )
    local_heads = new_keys.shape[1]
    queries = queries.reshape(local_rows, local_heads, -1, HEAD_DIM)
    usable = jnp.arange(cache_k.shape[2], dtype=jnp.int32)[None, :] < lengths[:, None]
    attended = jax.vmap(attend_one, in_axes=(1, 1, 1, 1, 1, None), out_axes=1)(
        queries, new_keys, new_values, cache_k, cache_v, usable
    )
    attended = attended.reshape(local_rows, query_width)
    all_heads = lax.all_gather(attended, "gy", axis=0, tiled=True)
    row_slab = all_heads
    attention_output = lax.psum_scatter(
        jnp.dot(row_slab, w_out, preferred_element_type=jnp.float32),
        "gx",
        scatter_dimension=0,
        tiled=True,
    )
    after_attention = (residual + attention_output).astype(jnp.bfloat16)
    mlp_tokens = normalize_rows(after_attention.astype(jnp.float32), mlp_gain)
    hidden_width = w_gate.shape[1]
    row_slab = mlp_tokens
    summed = lax.psum_scatter(
        jnp.concatenate(
            [
                jnp.dot(row_slab, w_gate, preferred_element_type=jnp.float32),
                jnp.dot(row_slab, w_up, preferred_element_type=jnp.float32),
            ],
            axis=1,
        ),
        "gy",
        scatter_dimension=0,
        tiled=True,
    )
    local_activation = (jax.nn.silu(summed[:, :hidden_width]) * summed[:, hidden_width:]).astype(
        jnp.bfloat16
    )
    activation = lax.all_gather(local_activation, "gy", axis=0, tiled=True)
    row_slab = activation
    down_sum = lax.psum_scatter(
        jnp.dot(row_slab, w_down, preferred_element_type=jnp.float32),
        "gx",
        scatter_dimension=0,
        tiled=True,
    )
    after_mlp = (after_attention.astype(jnp.float32) + down_sum).astype(jnp.bfloat16)
    final_tokens = normalize_rows(after_mlp.astype(jnp.float32), final_gain)
    row_slab = final_tokens
    logits = lax.psum_scatter(
        jnp.dot(row_slab, w_head, preferred_element_type=jnp.float32),
        "gy",
        scatter_dimension=0,
        tiled=True,
    )
    vocab_local = logits.shape[1]
    vocab_start = lax.axis_index("gx") * vocab_local
    chosen = jnp.arange(vocab_local, dtype=jnp.int32)[None, :] + vocab_start == draft_ids[:, None]
    picked_local = jnp.sum(jnp.where(chosen, logits, 0.0), axis=1)
    local_top = jnp.max(logits, axis=1)
    local_sum = jnp.sum(jnp.exp(logits - local_top[:, None]), axis=1)
    highest, exp_total, picked = combined_all(
        (local_top, local_sum, picked_local), "gx", combine_totals
    )
    normalizer = highest + jnp.log(exp_total)
    return (logits - normalizer[:, None], picked - normalizer)


def solution(mesh):
    return jax.shard_map(
        shards,
        mesh=mesh,
        in_specs=(
            P("gx", "gy"),
            P("gy"),
            P("gy"),
            P("gy"),
            P("gy", "gx"),
            P("gy", "gx"),
            P("gy", "gx"),
            P("gx", "gy"),
            P("gy", "gx", None, None),
            P("gy", "gx", None, None),
            P("gy"),
            P("gy", "gx"),
            P("gy", "gx"),
            P("gx", "gy"),
            P("gy"),
            P("gy", "gx"),
        ),
        out_specs=(P("gy", "gx"), P("gy")),
        check_vma=False,
    )
```

profile of v0, /device:TPU:0, one launch (start us, length us, event | category | flops | bytes accessed | tf_op | source)
XLA Modules:
  0.0 791.5 jit_solution(4075788909980705325)
XLA Ops:
  9.0 23.1 %psum.21 = f32[64]{0:T(128)S(1)} all-reduce(f32[64]{0:T(128)S(1)} %fusion.33), channel_id=1, replica_groups=mesh['gx'=4,'gy'=8] {'gy'}, use_global_device_ids=true, to_apply=%region_1.0 | all-reduce | flops 64 | bytes 512 | tf_op jit(solution)/shard_map/psum | solution.py:41
  33.2 7.2 all_gather.33
  40.4 3.5 fusion.55
  46.6 67.2 %reduce-scatter.6.cloned.1.call-done = f32[32,2560]{1,0:T(8,128)} async-done(((f32[256,2560]{1,0:T(8,128)}), f32[32,2560]{1,0:T(8,128)}) %reduce-scatter.6.cloned.1.call-update) | async-done | bytes 327696 | tf_op jit(solution)/shard_map/reduce_scatter | solution.py:98
  116.4 5.1 fusion.54
  123.1 4.0 fusion.23
  127.9 39.5 %all-gather.6.cloned.1.call-done = bf16[256,2048]{1,0:T(8,128)(2,1)} async-done(((bf16[32,2048]{1,0:T(8,128)(2,1)}), bf16[256,2048]{1,0:T(8,128)(2,1)}) %all-gather.6.cloned.1.call-update) | async-done | bytes 1048592 | tf_op jit(solution)/shard_map/all_gather | solution.py:134
  167.4 4.8 fusion.58
  172.3 23.6 %reduce-scatter.8.cloned.1.call-done = f32[64,1024]{1,0:T(8,128)} async-done(((f32[256,1024]{1,0:T(8,128)}), f32[64,1024]{1,0:T(8,128)}) %reduce-scatter.8.cloned.1.call-update) | async-done | bytes 262160 | tf_op jit(solution)/shard_map/reduce_scatter | solution.py:136
  197.0 21.4 %psum.22 = f32[64]{0:T(128)S(1)} all-reduce(f32[64]{0:T(128)S(1)} %get-tuple-element.206), channel_id=1, replica_groups=mesh['gx'=4,'gy'=8] {'gy'}, use_global_device_ids=true, to_apply=%region_7.8 | all-reduce | flops 64 | bytes 512 | tf_op jit(solution)/shard_map/psum | solution.py:41
  218.5 6.7 all_gather.35
  225.2 7.4 fusion.59
  234.0 4.1 fusion.60
  238.1 5.5 pad_maximum_fusion
  243.6 233.7 %reduce-scatter.10.cloned.1.call-done = f32[32,14336]{1,0:T(8,128)} async-done(((f32[256,14336]{1,0:T(8,128)}), f32[32,14336]{1,0:T(8,128)}) %reduce-scatter.10.cloned.1.call-update) | async-done | bytes 1835024 | tf_op jit(solution)/shard_map/reduce_scatter | solution.py:146
  477.4 2.5 fusion.26
  479.9 65.4 %all-gather.8.cloned.1.call-done = bf16[256,7168]{1,0:T(8,128)(2,1)} async-done(((bf16[32,7168]{1,0:T(8,128)(2,1)}), bf16[256,7168]{1,0:T(8,128)(2,1)}) %all-gather.8.cloned.1.call-update) | async-done | bytes 3670032 | tf_op jit(solution)/shard_map/all_gather | solution.py:161
  545.3 11.2 %fusion.61 = f32[256,1024]{1,0:T(8,128)} fusion(bf16[256,7168]{1,0:T(8,128)(2,1)} %all-gather.8.cloned.1.call-done, bf16[7168,1024]{1,0:T(8,128)(2,1)} %param.31), kind=kOutput, calls=%fused_computation.92 | convolution fusion | flops 3758096384 | bytes 19398656 | tf_op jit(solution)/shard_map/dot_general | solution.py:164
  556.6 23.6 %reduce-scatter.12.cloned.1.call-done = f32[64,1024]{1,0:T(8,128)} async-done(((f32[256,1024]{1,0:T(8,128)}), f32[64,1024]{1,0:T(8,128)}) %reduce-scatter.12.cloned.1.call-update) | async-done | bytes 262160 | tf_op jit(solution)/shard_map/reduce_scatter | solution.py:163
  581.3 21.4 %psum.23 = f32[64]{0:T(128)S(1)} all-reduce(f32[64]{0:T(128)S(1)} %fusion.30), channel_id=1, replica_groups=mesh['gx'=4,'gy'=8] {'gy'}, use_global_device_ids=true, to_apply=%region_11.12 | all-reduce | flops 64 | bytes 512 | tf_op jit(solution)/shard_map/psum | solution.py:41
  603.8 6.7 all_gather.37
  610.5 18.4 %fusion.62 = f32[256,8000]{1,0:T(8,128)} fusion(bf16[256,1024]{1,0:T(8,128)(2,1)S(1)} %all_gather.37, bf16[1024,8000]{0,1:T(8,128)(2,1)} %param.33), kind=kOutput, calls=%fused_computation.93 | convolution fusion | flops 4194304000 | bytes 25100288 | tf_op jit(solution)/shard_map/dot_general | solution.py:173
  630.8 141.3 %reduce-scatter.14.cloned.1.call-done = f32[32,8000]{1,0:T(8,128)} async-done(((f32[256,8000]{1,0:T(8,128)}), f32[32,8000]{1,0:T(8,128)}) %reduce-scatter.14.cloned.1.call-update) | async-done | bytes 1024016 | tf_op jit(solution)/shard_map/reduce_scatter | solution.py:172
  775.8 5.6 all-reduce.3
  (101 shorter events, 23.6 us)
Async XLA Ops:
  7.2 36.7 %copy-start = (bf16[1024,256]{1,0:T(8,128)(2,1)S(1)}, bf16[1024,256]{1,0:T(8,128)(2,1)}, u32[]{:S(2)}) copy-start(bf16[1024,256]{1,0:T(8,128)(2,1)} %param.23) | copy-start | bytes 1572868
  7.2 37.0 %copy-start.3 = (bf16[1024,256]{1,0:T(8,128)(2,1)S(1)}, bf16[1024,256]{1,0:T(8,128)(2,1)}, u32[]{:S(2)}) copy-start(bf16[1024,256]{1,0:T(8,128)(2,1)} %param.24) | copy-start | bytes 1572868
  7.2 106.6 %reduce-scatter.6.cloned.1.call-start = ((), (), s32[]{:S(2)}) async-start(), calls=%async_computation.5 | async-start | bytes 2949120 | tf_op jit(solution)/shard_map/reduce_scatter | solution.py:98
  43.9 2.5 copy-start.7
  46.3 121.2 %all-gather.6.cloned.1.call-start = ((), (), s32[]{:S(2)}) async-start(), calls=%async_computation.6 | async-start | bytes 1179648 | tf_op jit(solution)/shard_map/all_gather | solution.py:134
  127.1 45.2 %copy-start.4 = (bf16[1024]{0:T(1024)(128)(2,1)S(1)}, bf16[1024]{0:T(1024)(128)(2,1)}, u32[]{:S(2)}) copy-start(bf16[1024]{0:T(1024)(128)(2,1)} %param.28) | copy-start | bytes 6148
  127.1 68.8 %copy-start.2 = (bf16[64,1024]{1,0:T(8,128)(2,1)S(1)}, bf16[64,1024]{1,0:T(8,128)(2,1)}, u32[]{:S(2)}) copy-start(bf16[64,1024]{1,0:T(8,128)(2,1)} %param.18) | copy-start | bytes 393220
  127.9 68.0 %reduce-scatter.8.cloned.1.call-start = ((), (), s32[]{:S(2)}) async-start(), calls=%async_computation.7 | async-start | bytes 1310720 | tf_op jit(solution)/shard_map/reduce_scatter | solution.py:136
  172.2 60.4 %slice-start = ((s8[14680064]{0:T(1024)(128)(4,1)}), s8[2097152]{0:T(1024)(128)(4,1)S(1)}, s32[]{:S(2)}) async-start(s8[14680064]{0:T(1024)(128)(4,1)} %bitcast.94), calls=%async_computation.12 | async-start | bytes 4194304
  172.2 305.1 %reduce-scatter.10.cloned.1.call-start = ((), (), s32[]{:S(2)}) async-start(), calls=%async_computation.8 | async-start | bytes 16515072 | tf_op jit(solution)/shard_map/reduce_scatter | solution.py:146
  225.2 7.4 slice-start.1
  225.2 7.6 slice-start.2
  225.2 8.8 %slice-start.3 = ((s8[14680064]{0:T(1024)(128)(4,1)}), s8[4194304]{0:T(1024)(128)(4,1)S(1)}, s32[]{:S(2)}) async-start(s8[14680064]{0:T(1024)(128)(4,1)} %bitcast.94), calls=%async_computation.15 | async-start | bytes 8388608
  243.6 301.8 %all-gather.8.cloned.1.call-start = ((), (), s32[]{:S(2)}) async-start(), calls=%async_computation.9 | async-start | bytes 4128768 | tf_op jit(solution)/shard_map/all_gather | solution.py:161
  479.9 76.7 %copy-start.5 = (bf16[1024]{0:T(1024)(128)(2,1)S(1)}, bf16[1024]{0:T(1024)(128)(2,1)}, u32[]{:S(2)}) copy-start(bf16[1024]{0:T(1024)(128)(2,1)} %param.32) | copy-start | bytes 6148
  479.9 100.3 %reduce-scatter.12.cloned.1.call-start = ((), (), s32[]{:S(2)}) async-start(), calls=%async_computation.10 | async-start | bytes 1310720 | tf_op jit(solution)/shard_map/reduce_scatter | solution.py:163
  556.6 215.5 %reduce-scatter.14.cloned.1.call-start = ((), (), s32[]{:S(2)}) async-start(), calls=%async_computation.11 | async-start | bytes 9289728 | tf_op jit(solution)/shard_map/reduce_scatter | solution.py:172
  628.9 0.7 copy-start.8
  628.9 144.8 %copy-start.6 = (s32[32]{0:T(128)S(1)}, s32[32]{0:T(128)}, u32[]{:S(2)}) copy-start(s32[32]{0:T(128)} %param.20) | copy-start | bytes 388
  628.9 155.7 %copy-start.1 = (bf16[1024,256]{1,0:T(8,128)(2,1)S(1)}, bf16[1024,256]{1,0:T(8,128)(2,1)}, u32[]{:S(2)}) copy-start(bf16[1024,256]{1,0:T(8,128)(2,1)} %param.23) | copy-start | bytes 1572868
Sparse Core Ops, SparseCore 0:
  46.4 67.3 reduce-scatter.5
  128.0 39.4 all-gather.5
  172.3 23.4 reduce-scatter.7
  243.7 233.6 reduce-scatter.9
  480.0 65.3 all-gather.7
  556.7 23.4 reduce-scatter.11
  629.1 142.9 reduce-scatter.13
where the time goes:
time: 792 us
  waiting for transfers between devices  594 us (75%)
  blocking collectives  92.1 us (12%)
  matrix products  59.3 us (7%)
  other arithmetic  23.6 us (3%)
  between operations  15.1 us (2%)
    reduce_scatter x1, waiting for transfers between devices, shards(): lax.psum_scatter(jnp.concatenate([jnp.dot(row_slab, w_gate, preferred_ele...  234 us
    reduce_scatter x1, waiting for transfers between devices, shards(): lax.psum_scatter(jnp.dot(row_slab, w_head, preferred_element_type=jnp.flo...  141 us
    reduce_scatter x1, waiting for transfers between devices, shards(): lax.psum_scatter(jnp.concatenate([jnp.dot(row_slab, w_query, preferred_el...  67.2 us
    psum x3, blocking collectives, normalize_rows(): squares = lax.psum(jnp.sum(activity * activity, axis=1), 'gy')  65.9 us
    all_gather x1, waiting for transfers between devices, shards(): activation = lax.all_gather(local_activation, 'gy', axis=0, tiled=True)  65.4 us
    all_gather x1, waiting for transfers between devices, shards(): all_heads = lax.all_gather(attended, 'gy', axis=0, tiled=True)  39.5 us
    reduce_scatter x1, waiting for transfers between devices, shards(): lax.psum_scatter(jnp.dot(row_slab, w_down, preferred_element_type=jnp.flo...  23.6 us
    reduce_scatter x1, waiting for transfers between devices, shards(): lax.psum_scatter(jnp.dot(row_slab, w_out, preferred_element_type=jnp.floa...  23.6 us
  transfers between devices with their start and end apart: 7, of which 7 were waited for; matrix products, arithmetic and copies ran while one was open for 0% of the time, Pallas kernels for 0%

commit v1 on v0

--- a/solution.py
+++ b/solution.py
@@ -158,7 +158,12 @@
     local_activation = (jax.nn.silu(summed[:, :hidden_width]) * summed[:, hidden_width:]).astype(
         jnp.bfloat16
     )
-    activation = lax.all_gather(local_activation, "gy", axis=0, tiled=True)
+    ring = [local_activation]
+    for hop in range(7):
+        ring.append(lax.ppermute(ring[-1], "gy", [(dev, (dev + 1) % 8) for dev in range(8)]))
+    activation = jnp.roll(
+        jnp.concatenate(ring[::-1], axis=0), (lax.axis_index("gy") + 1) * ring[0].shape[0], axis=0
+    )
     row_slab = activation
     down_sum = lax.psum_scatter(
         jnp.dot(row_slab, w_down, preferred_element_type=jnp.float32),

time: 792 us -> 819 us (1.034)
  waiting for transfers between devices: 594 us -> 614 us
    ppermute x0 -> x7, waiting for transfers between devices: none -> 87.3 us  [shards(): lax.ppermute(ring[-1], 'gy', [(dev, (dev + 1) % 8) for dev in range(8)])]
    all_gather x1 -> x0, waiting for transfers between devices: 65.4 us -> none  [shards(): activation = lax.all_gather(local_activation, 'gy', axis=0, tiled=True)]
  transfers between devices with their start and end apart: 7 -> 13, of which waited for: 7 -> 13; matrix products, arithmetic and copies ran while one was open for 0% -> 0% of each run, Pallas kernels for 0% -> 0%
where the time goes in v1:
time: 819 us; the launch traced here: 818 us
  waiting for transfers between devices  614 us (75%)
  blocking collectives  92.1 us (11%)
  matrix products  56.5 us (7%)
  other arithmetic  23.5 us (3%)
  between operations  15.2 us (2%)
  local copies, waits for them, and re-layouts  14.7 us (2%)
    reduce_scatter x1, waiting for transfers between devices, shards(): lax.psum_scatter(jnp.concatenate([jnp.dot(row_slab, w_gate, preferred_ele...  234 us
    reduce_scatter x1, waiting for transfers between devices, shards(): lax.psum_scatter(jnp.dot(row_slab, w_head, preferred_element_type=jnp.flo...  141 us
    ppermute x7, waiting for transfers between devices, shards(): lax.ppermute(ring[-1], 'gy', [(dev, (dev + 1) % 8) for dev in range(8)])  87.3 us
    reduce_scatter x1, waiting for transfers between devices, shards(): lax.psum_scatter(jnp.concatenate([jnp.dot(row_slab, w_query, preferred_el...  67.3 us
    psum x3, blocking collectives, normalize_rows(): squares = lax.psum(jnp.sum(activity * activity, axis=1), 'gy')  65.9 us
    all_gather x1, waiting for transfers between devices, shards(): all_heads = lax.all_gather(attended, 'gy', axis=0, tiled=True)  39.5 us
    reduce_scatter x1, waiting for transfers between devices, shards(): lax.psum_scatter(jnp.dot(row_slab, w_out, preferred_element_type=jnp.floa...  23.6 us
    reduce_scatter x1, waiting for transfers between devices, shards(): lax.psum_scatter(jnp.dot(row_slab, w_down, preferred_element_type=jnp.flo...  22 us
  transfers between devices with their start and end apart: 13, of which 13 were waited for; matrix products, arithmetic and copies ran while one was open for 0% of the time, Pallas kernels for 0%

profile of v1, /device:TPU:0, one launch (start us, length us, event | category | flops | bytes accessed | tf_op | source)
XLA Modules:
  0.0 818.3 jit_solution(15705087490672321216)
XLA Ops:
  9.0 23.1 %psum.21 = f32[64]{0:T(128)S(1)} all-reduce(f32[64]{0:T(128)S(1)} %fusion.35), channel_id=1, replica_groups=mesh['gx'=4,'gy'=8] {'gy'}, use_global_device_ids=true, to_apply=%region_1.0 | all-reduce | flops 64 | bytes 512 | tf_op jit(solution)/shard_map/psum | solution.py:41
  33.2 7.2 all_gather.30
  46.6 67.3 %reduce-scatter.6.cloned.1.call-done = f32[32,2560]{1,0:T(8,128)} async-done(((f32[256,2560]{1,0:T(8,128)}), f32[32,2560]{1,0:T(8,128)}) %reduce-scatter.6.cloned.1.call-update) | async-done | bytes 327696 | tf_op jit(solution)/shard_map/reduce_scatter | solution.py:98
  128.0 39.5 %all-gather.5.cloned.1.call-done = bf16[256,2048]{1,0:T(8,128)(2,1)} async-done(((bf16[32,2048]{1,0:T(8,128)(2,1)}), bf16[256,2048]{1,0:T(8,128)(2,1)}) %all-gather.5.cloned.1.call-update) | async-done | bytes 1048592 | tf_op jit(solution)/shard_map/all_gather | solution.py:134
  172.3 23.6 %reduce-scatter.8.cloned.1.call-done = f32[64,1024]{1,0:T(8,128)} async-done(((f32[256,1024]{1,0:T(8,128)}), f32[64,1024]{1,0:T(8,128)}) %reduce-scatter.8.cloned.1.call-update) | async-done | bytes 262160 | tf_op jit(solution)/shard_map/reduce_scatter | solution.py:136
  197.0 21.4 %psum.22 = f32[64]{0:T(128)S(1)} all-reduce(f32[64]{0:T(128)S(1)} %get-tuple-element.206), channel_id=1, replica_groups=mesh['gx'=4,'gy'=8] {'gy'}, use_global_device_ids=true, to_apply=%region_7.8 | all-reduce | flops 64 | bytes 512 | tf_op jit(solution)/shard_map/psum | solution.py:41
  218.5 6.7 all_gather.32
  225.2 7.4 fusion.62
  238.1 5.5 pad_maximum_fusion
  243.6 233.8 %reduce-scatter.10.cloned.1.call-done = f32[32,14336]{1,0:T(8,128)} async-done(((f32[256,14336]{1,0:T(8,128)}), f32[32,14336]{1,0:T(8,128)}) %reduce-scatter.10.cloned.1.call-update) | async-done | bytes 1835024 | tf_op jit(solution)/shard_map/reduce_scatter | solution.py:146
  480.8 13.4 %collective-permute-done = bf16[32,7168]{1,0:T(8,128)(2,1)S(1)} collective-permute-done((bf16[32,7168]{1,0:T(8,128)(2,1)S(1)}, bf16[32,7168]{1,0:T(8,128)(2,1)S(1)}, u32[]{:S(2)}, u32[]{:S(2)}) %collective-permute-start) | collective-permute-done | bytes 458784 | tf_op jit(solution)/shard_map/ppermute | solution.py:163
  494.2 14.0 %collective-permute-done.1 = bf16[32,7168]{1,0:T(8,128)(2,1)S(1)} collective-permute-done((bf16[32,7168]{1,0:T(8,128)(2,1)S(1)}, bf16[32,7168]{1,0:T(8,128)(2,1)S(1)}, u32[]{:S(2)}, u32[]{:S(2)}) %collective-permute-start.1) | collective-permute-done | bytes 458784 | tf_op jit(solution)/shard_map/ppermute | solution.py:163
  508.2 13.2 %collective-permute-done.2 = bf16[32,7168]{1,0:T(8,128)(2,1)S(1)} collective-permute-done((bf16[32,7168]{1,0:T(8,128)(2,1)S(1)}, bf16[32,7168]{1,0:T(8,128)(2,1)S(1)}, u32[]{:S(2)}, u32[]{:S(2)}) %collective-permute-start.2) | collective-permute-done | bytes 458784 | tf_op jit(solution)/shard_map/ppermute | solution.py:163
  521.4 12.3 %collective-permute-done.3 = bf16[32,7168]{1,0:T(8,128)(2,1)S(1)} collective-permute-done((bf16[32,7168]{1,0:T(8,128)(2,1)S(1)}, bf16[32,7168]{1,0:T(8,128)(2,1)S(1)}, u32[]{:S(2)}, u32[]{:S(2)}) %collective-permute-start.3) | collective-permute-done | bytes 458784 | tf_op jit(solution)/shard_map/ppermute | solution.py:163
  534.6 11.5 %collective-permute-done.4 = bf16[32,7168]{1,0:T(8,128)(2,1)S(1)} collective-permute-done((bf16[32,7168]{1,0:T(8,128)(2,1)S(1)}, bf16[32,7168]{1,0:T(8,128)(2,1)S(1)}, u32[]{:S(2)}, u32[]{:S(2)}) %collective-permute-start.4) | collective-permute-done | bytes 458784 | tf_op jit(solution)/shard_map/ppermute | solution.py:163
  546.8 11.3 %collective-permute-done.5 = bf16[32,7168]{1,0:T(8,128)(2,1)} collective-permute-done((bf16[32,7168]{1,0:T(8,128)(2,1)S(1)}, bf16[32,7168]{1,0:T(8,128)(2,1)}, u32[]{:S(2)}, u32[]{:S(2)}) %collective-permute-start.5) | collective-permute-done | bytes 458784 | tf_op jit(solution)/shard_map/ppermute | solution.py:163
  558.1 11.5 %collective-permute-done.6 = bf16[32,7168]{1,0:T(8,128)(2,1)} collective-permute-done((bf16[32,7168]{1,0:T(8,128)(2,1)}, bf16[32,7168]{1,0:T(8,128)(2,1)}, u32[]{:S(2)}, u32[]{:S(2)}) %collective-permute-start.6) | collective-permute-done | bytes 458784 | tf_op jit(solution)/shard_map/ppermute | solution.py:163
  576.8 8.3 %fusion.11 = f32[256,1024]{1,0:T(8,128)} fusion(bf16[7168,1024]{1,0:T(8,128)(2,1)} %param.31, bf16[512,7168]{1,0:T(8,128)(2,1)S(1)} %constant_dynamic-update-slice_fusion, s32[]{:T(128)S(6)} %select_n.35), kind=kOutput, calls=%fused_computation.15 | convolution fusion | flops 3758096384 | bytes 19398660 | tf_op jit(solution)/shard_map/dot_general | solution.py:169
  585.2 22.0 %reduce-scatter.12.cloned.1.call-done = f32[64,1024]{1,0:T(8,128)} async-done(((f32[256,1024]{1,0:T(8,128)}), f32[64,1024]{1,0:T(8,128)}) %reduce-scatter.12.cloned.1.call-update) | async-done | bytes 262160 | tf_op jit(solution)/shard_map/reduce_scatter | solution.py:168
  608.4 21.4 %psum.23 = f32[64]{0:T(128)S(1)} all-reduce(f32[64]{0:T(128)S(1)} %fusion.32), channel_id=1, replica_groups=mesh['gx'=4,'gy'=8] {'gy'}, use_global_device_ids=true, to_apply=%region_11.12 | all-reduce | flops 64 | bytes 512 | tf_op jit(solution)/shard_map/psum | solution.py:41
  630.8 6.7 all_gather.33
  637.5 18.5 %fusion.64 = f32[256,8000]{1,0:T(8,128)} fusion(bf16[256,1024]{1,0:T(8,128)(2,1)S(1)} %all_gather.33, bf16[1024,8000]{0,1:T(8,128)(2,1)} %param.33), kind=kOutput, calls=%fused_computation.111 | convolution fusion | flops 4194304000 | bytes 25100288 | tf_op jit(solution)/shard_map/dot_general | solution.py:178
  657.9 140.9 %reduce-scatter.14.cloned.1.call-done = f32[32,8000]{1,0:T(8,128)} async-done(((f32[256,8000]{1,0:T(8,128)}), f32[32,8000]{1,0:T(8,128)}) %reduce-scatter.14.cloned.1.call-update) | async-done | bytes 1024016 | tf_op jit(solution)/shard_map/reduce_scatter | solution.py:177
  802.6 5.6 all-reduce.3
  (138 shorter events, 57.0 us)
Async XLA Ops:
  7.2 36.7 %copy-start = (bf16[1024,256]{1,0:T(8,128)(2,1)S(1)}, bf16[1024,256]{1,0:T(8,128)(2,1)}, u32[]{:S(2)}) copy-start(bf16[1024,256]{1,0:T(8,128)(2,1)} %param.23) | copy-start | bytes 1572868
  7.2 37.0 %copy-start.8 = (bf16[1024,256]{1,0:T(8,128)(2,1)S(1)}, bf16[1024,256]{1,0:T(8,128)(2,1)}, u32[]{:S(2)}) copy-start(bf16[1024,256]{1,0:T(8,128)(2,1)} %param.24) | copy-start | bytes 1572868
  7.2 106.7 %reduce-scatter.6.cloned.1.call-start = ((), (), s32[]{:S(2)}) async-start(), calls=%async_computation.5 | async-start | bytes 2949120 | tf_op jit(solution)/shard_map/reduce_scatter | solution.py:98
  46.3 121.2 %all-gather.5.cloned.1.call-start = ((), (), s32[]{:S(2)}) async-start(), calls=%async_computation.6 | async-start | bytes 1179648 | tf_op jit(solution)/shard_map/all_gather | solution.py:134
  123.1 49.2 %copy-start.9 = (bf16[1024]{0:T(1024)(128)(2,1)S(1)}, bf16[1024]{0:T(1024)(128)(2,1)}, u32[]{:S(2)}) copy-start(bf16[1024]{0:T(1024)(128)(2,1)} %param.28) | copy-start | bytes 6148
  123.1 72.8 %copy-start.7 = (bf16[64,1024]{1,0:T(8,128)(2,1)S(1)}, bf16[64,1024]{1,0:T(8,128)(2,1)}, u32[]{:S(2)}) copy-start(bf16[64,1024]{1,0:T(8,128)(2,1)} %param.18) | copy-start | bytes 393220
  127.9 68.0 %reduce-scatter.8.cloned.1.call-start = ((), (), s32[]{:S(2)}) async-start(), calls=%async_computation.7 | async-start | bytes 1310720 | tf_op jit(solution)/shard_map/reduce_scatter | solution.py:136
  172.2 60.4 %slice-start = ((s8[14680064]{0:T(1024)(128)(4,1)}), s8[2097152]{0:T(1024)(128)(4,1)S(1)}, s32[]{:S(2)}) async-start(s8[14680064]{0:T(1024)(128)(4,1)} %bitcast.93), calls=%async_computation.11 | async-start | bytes 4194304
  172.2 305.1 %reduce-scatter.10.cloned.1.call-start = ((), (), s32[]{:S(2)}) async-start(), calls=%async_computation.8 | async-start | bytes 16515072 | tf_op jit(solution)/shard_map/reduce_scatter | solution.py:146
  225.2 8.8 %slice-start.3 = ((s8[14680064]{0:T(1024)(128)(4,1)}), s8[4194304]{0:T(1024)(128)(4,1)S(1)}, s32[]{:S(2)}) async-start(s8[14680064]{0:T(1024)(128)(4,1)} %bitcast.93), calls=%async_computation.14 | async-start | bytes 8388608
  243.6 363.7 %reduce-scatter.12.cloned.1.call-start = ((), (), s32[]{:S(2)}) async-start(), calls=%async_computation.9 | async-start | bytes 1310720 | tf_op jit(solution)/shard_map/reduce_scatter | solution.py:168
  477.4 96.6 %copy-start.2 = (f32[32,14336]{1,0:T(8,128)S(1)}, f32[32,14336]{1,0:T(8,128)}, u32[]{:S(2)}) copy-start(f32[32,14336]{1,0:T(8,128)} %reduce-scatter.10.cloned.1.call-done) | copy-start | bytes 5505028
  479.2 15.0 %collective-permute-start = (bf16[32,7168]{1,0:T(8,128)(2,1)S(1)}, bf16[32,7168]{1,0:T(8,128)(2,1)S(1)}, u32[]{:S(2)}, u32[]{:S(2)}) collective-permute-start(bf16[32,7168]{1,0:T(8,128)(2,1)S(1)} %fusion.28), channel_id=1, source_target_pairs={{0,1},{1,2},{2,3},{3,4},{4,5},{5,6},{6,7},{7,0},{8,9},{9,10},{10,1... | collective-permute-start | bytes 1376264 | tf_op jit(solution)/shard_map/ppermute | solution.py:163
  494.2 14.1 %collective-permute-start.1 = (bf16[32,7168]{1,0:T(8,128)(2,1)S(1)}, bf16[32,7168]{1,0:T(8,128)(2,1)S(1)}, u32[]{:S(2)}, u32[]{:S(2)}) collective-permute-start(bf16[32,7168]{1,0:T(8,128)(2,1)S(1)} %collective-permute-done), channel_id=1, source_target_pairs={{0,1},{1,2},{2,3},{3,4},{4,5},{5,6},{6,7},{7,0},{8,9},{9,10},{10,1... | collective-permute-start | bytes 1376264 | tf_op jit(solution)/shard_map/ppermute | solution.py:163
  508.2 13.2 %collective-permute-start.2 = (bf16[32,7168]{1,0:T(8,128)(2,1)S(1)}, bf16[32,7168]{1,0:T(8,128)(2,1)S(1)}, u32[]{:S(2)}, u32[]{:S(2)}) collective-permute-start(bf16[32,7168]{1,0:T(8,128)(2,1)S(1)} %collective-permute-done.1), channel_id=1, source_target_pairs={{0,1},{1,2},{2,3},{3,4},{4,5},{5,6},{6,7},{7,0},{8,9},{9,10},{10,1... | collective-permute-start | bytes 1376264 | tf_op jit(solution)/shard_map/ppermute | solution.py:163
  521.4 12.3 %collective-permute-start.3 = (bf16[32,7168]{1,0:T(8,128)(2,1)S(1)}, bf16[32,7168]{1,0:T(8,128)(2,1)S(1)}, u32[]{:S(2)}, u32[]{:S(2)}) collective-permute-start(bf16[32,7168]{1,0:T(8,128)(2,1)S(1)} %collective-permute-done.2), channel_id=1, source_target_pairs={{0,1},{1,2},{2,3},{3,4},{4,5},{5,6},{6,7},{7,0},{8,9},{9,10},{10,1... | collective-permute-start | bytes 1376264 | tf_op jit(solution)/shard_map/ppermute | solution.py:163
  534.6 11.5 %collective-permute-start.4 = (bf16[32,7168]{1,0:T(8,128)(2,1)S(1)}, bf16[32,7168]{1,0:T(8,128)(2,1)S(1)}, u32[]{:S(2)}, u32[]{:S(2)}) collective-permute-start(bf16[32,7168]{1,0:T(8,128)(2,1)S(1)} %collective-permute-done.3), channel_id=1, source_target_pairs={{0,1},{1,2},{2,3},{3,4},{4,5},{5,6},{6,7},{7,0},{8,9},{9,10},{10,1... | collective-permute-start | bytes 1376264 | tf_op jit(solution)/shard_map/ppermute | solution.py:163
  546.8 11.3 %collective-permute-start.5 = (bf16[32,7168]{1,0:T(8,128)(2,1)S(1)}, bf16[32,7168]{1,0:T(8,128)(2,1)}, u32[]{:S(2)}, u32[]{:S(2)}) collective-permute-start(bf16[32,7168]{1,0:T(8,128)(2,1)S(1)} %collective-permute-done.4), channel_id=1, source_target_pairs={{0,1},{1,2},{2,3},{3,4},{4,5},{5,6},{6,7},{7,0},{8,9},{9,10},{10,1... | collective-permute-start | bytes 1376264 | tf_op jit(solution)/shard_map/ppermute | solution.py:163
  558.1 11.5 %collective-permute-start.6 = (bf16[32,7168]{1,0:T(8,128)(2,1)}, bf16[32,7168]{1,0:T(8,128)(2,1)}, u32[]{:S(2)}, u32[]{:S(2)}) collective-permute-start(bf16[32,7168]{1,0:T(8,128)(2,1)} %collective-permute-done.5), channel_id=1, source_target_pairs={{0,1},{1,2},{2,3},{3,4},{4,5},{5,6},{6,7},{7,0},{8,9},{9,10},{10,1... | collective-permute-start | bytes 1376264 | tf_op jit(solution)/shard_map/ppermute | solution.py:163
  558.1 18.2 %copy-start.6 = (bf16[32,7168]{1,0:T(8,128)(2,1)S(1)}, bf16[32,7168]{1,0:T(8,128)(2,1)}, u32[]{:S(2)}) copy-start(bf16[32,7168]{1,0:T(8,128)(2,1)} %copy-done.5) | copy-start | bytes 1376260
  558.1 18.2 %copy-start.4 = (bf16[32,7168]{1,0:T(8,128)(2,1)S(1)}, bf16[32,7168]{1,0:T(8,128)(2,1)}, u32[]{:S(2)}) copy-start(bf16[32,7168]{1,0:T(8,128)(2,1)} %copy-done.3) | copy-start | bytes 1376260
  585.1 213.7 %reduce-scatter.14.cloned.1.call-start = ((), (), s32[]{:S(2)}) async-start(), calls=%async_computation.10 | async-start | bytes 9289728 | tf_op jit(solution)/shard_map/reduce_scatter | solution.py:177
  637.5 173.9 %copy-start.1 = (bf16[1024,256]{1,0:T(8,128)(2,1)S(1)}, bf16[1024,256]{1,0:T(8,128)(2,1)}, u32[]{:S(2)}) copy-start(bf16[1024,256]{1,0:T(8,128)(2,1)} %param.23) | copy-start | bytes 1572868
  656.0 144.5 %copy-start.11 = (s32[32]{0:T(128)S(1)}, s32[32]{0:T(128)}, u32[]{:S(2)}) copy-start(s32[32]{0:T(128)} %param.20) | copy-start | bytes 388
  (7 other events, 31.6 us)
Sparse Core Ops, SparseCore 0:
  46.4 67.3 reduce-scatter.5
  128.1 39.3 all-gather.4
  172.4 23.4 reduce-scatter.7
  243.7 233.6 reduce-scatter.9
  585.3 21.9 reduce-scatter.11
  656.2 142.6 reduce-scatter.13
